TPU v7x, 32 devices: a whole 2x2x4 slice. The times are simulated.
32 devices in a mesh: wide: 8 (over y, x, core), narrow: 4 (over z).
Axes of the slice: x: 2, y: 2, z: 4, core: 2. Of those that a mesh axis runs over, the one named last changes fastest.
Arguments:
- tokens: bfloat16 [32, 1536, 768], P(('wide', 'narrow')), may hold values from -6 to 6
- lengths: int32 [8, 4], P('wide'), may hold values from 1 to 1536, 4608 in all within a row
- qkv_weight: bfloat16 [768, 3, 768], P(None, None, 'narrow'), may hold values from -0.3125 to 0.3125
- qkv_bias: bfloat16 [3, 768], P(None, 'narrow'), may hold values from -3 to 3
- out_weight: bfloat16 [768, 768], P('narrow'), may hold values from -2.5 to 2.5
- out_bias: bfloat16 [768], replicated, may hold values from -2 to 2
- norm1_gain: bfloat16 [768], replicated, may hold values from 0.099609375 to 1.8984375
- norm1_shift: bfloat16 [768], replicated, may hold values from -2 to 2
- up_weight: bfloat16 [768, 3072], P(None, 'narrow'), may hold values from -0.21875 to 0.21875
- up_bias: bfloat16 [3072], P('narrow'), may hold values from -2 to 2
- down_weight: bfloat16 [3072, 768], P('narrow'), may hold values from -0.109375 to 0.109375
- down_bias: bfloat16 [768], replicated, may hold values from -2 to 2
- norm2_gain: bfloat16 [768], replicated, may hold values from 0.099609375 to 1.8984375
- norm2_shift: bfloat16 [768], replicated, may hold values from -2 to 2
- cotangent: bfloat16 [32, 1536, 768], P(('wide', 'narrow')), may hold values from -6 to 6
Outputs:
- output: bfloat16 [32, 1536, 768], P(('wide', 'narrow'))
- input_grad: float32 [32, 1536, 768], P(('wide', 'narrow'))
- grad_qkv_weight: float32 [768, 3, 768], P(None, None, 'narrow')
- grad_qkv_bias: float32 [3, 768], P(None, 'narrow')
- grad_out_weight: float32 [768, 768], P('narrow')
- grad_out_bias: float32 [768], replicated
- grad_norm1_gain: float32 [768], replicated
- grad_norm1_shift: float32 [768], replicated
- grad_up_weight: float32 [768, 3072], P(None, 'narrow')
- grad_up_bias: float32 [3072], P('narrow')
- grad_down_weight: float32 [3072, 768], P('narrow')
- grad_down_bias: float32 [768], replicated
- grad_norm2_gain: float32 [768], replicated
- grad_norm2_shift: float32 [768], replicated
Inputs may be any that keep to these rules, and one draw needn't show every extreme that they name: The 4 lengths of each wide index sum to 4608; positions at or beyond a slot's length are keys that no query attends to.
All inputs are finite; a program needn't handle non-finite values.
Results may differ from a plain program's by a relative error of at most 0.018.
The roundings to bfloat16 on the way count: a program that leaves them out, or rounds other values in their place, can miss the bound.
Values may be sent and summed in bfloat16 or wider, within the bound.
No kernel may reach another device: no remote copies, remote signals or barrier semaphores. Data moves between devices by JAX's collectives and lax.ppermute only.
A program may use at most 256 MiB of HBM per device.

v0:
```python
import jax
import jax.numpy as jnp
from jax import lax
from jax.sharding import PartitionSpec as P

HEADS = 12
HD = 64
NORM_EPS = 1e-06
MASK_VALUE = -1000000000.0


def rotary_tables(capacity, head_dim):
    positions = jnp.arange(capacity).astype(jnp.float32)
    frequencies = 10000.0 ** (-2.0 * jnp.arange(head_dim // 2).astype(jnp.float32) / head_dim)
    angles = positions[:, None] * frequencies[None, :]
    return (jnp.cos(angles)[:, None, :], jnp.sin(angles)[:, None, :])


def rotate(values, cosine, sine):
    half_dim = values.shape[-1] // 2
    first_half = values[..., :half_dim]
    second_half = values[..., half_dim:]
    return jnp.concatenate(
        [first_half * cosine - second_half * sine, second_half * cosine + first_half * sine],
        axis=-1,
    )


def norm_forward(values, gain_vec, shift_vec):
    row_mean = jnp.mean(values, axis=-1, keepdims=True)
    centred = values - row_mean
    inv_std = lax.rsqrt(jnp.mean(centred * centred, axis=-1, keepdims=True) + NORM_EPS)
    normed = centred * inv_std
    return (normed * gain_vec + shift_vec, normed, inv_std)


def norm_backward(upstream, normed, inv_std, gain_vec):
    scaled = upstream * gain_vec
    inner = (
        scaled
        - jnp.mean(scaled, axis=-1, keepdims=True)
        - normed * jnp.mean(scaled * normed, axis=-1, keepdims=True)
    )
    gain_grad = jnp.sum(upstream * normed, axis=(0, 1))
    shift_grad = jnp.sum(upstream, axis=(0, 1))
    return (inv_std * inner, gain_grad, shift_grad)


def to_items(values, group_count):
    slot_count, capacity, head_count, head_dim = values.shape
    values = values.reshape(slot_count, capacity, group_count, head_count // group_count, head_dim)
    values = values.transpose(0, 2, 1, 3, 4)
    return values.reshape(slot_count * group_count, capacity, head_count // group_count, head_dim)


def from_items(values, group_count):
    item_count, capacity, group_heads, head_dim = values.shape
    values = values.reshape(item_count // group_count, group_count, capacity, group_heads, head_dim)
    values = values.transpose(0, 2, 1, 3, 4)
    return values.reshape(item_count // group_count, capacity, group_count * group_heads, head_dim)


def attend_forward(query_item, key_item, value_item, item_length, block_rows, score_scale):
    capacity = query_item.shape[0]
    live_keys = jnp.arange(capacity) < item_length

    def one_block(offset):
        query_block = lax.dynamic_slice_in_dim(query_item, offset, block_rows, 0)
        scores = (
            jnp.einsum("qhe,khe->hqk", query_block, key_item, preferred_element_type=jnp.float32)
            * score_scale
        )
        scores = jnp.where(live_keys[None, None, :], scores, MASK_VALUE)
        row_max = jnp.max(scores, axis=-1, keepdims=True)
        exponentials = jnp.exp(scores - row_max)
        denominator = jnp.sum(exponentials, axis=-1, keepdims=True)
        weights = (exponentials / denominator).astype(jnp.bfloat16)
        context = jnp.einsum(
            "hqk,khe->qhe", weights, value_item, preferred_element_type=jnp.float32
        )
        return (context, (row_max + jnp.log(denominator))[..., 0])

    offsets = jnp.arange(capacity // block_rows) * block_rows
    context, log_sums = lax.map(one_block, offsets)
    return (context.reshape(query_item.shape), log_sums)


def attend_backward(
    query_item, key_item, value_item, grad_item, log_sums, item_length, block_rows, score_scale
):
    capacity = query_item.shape[0]
    live_keys = jnp.arange(capacity) < item_length

    def one_block(carry, inputs):
        key_grad, value_grad = carry
        offset, block_sums = inputs
        query_block = lax.dynamic_slice_in_dim(query_item, offset, block_rows, 0)
        grad_block = lax.dynamic_slice_in_dim(grad_item, offset, block_rows, 0)
        scores = (
            jnp.einsum("qhe,khe->hqk", query_block, key_item, preferred_element_type=jnp.float32)
            * score_scale
        )
        scores = jnp.where(live_keys[None, None, :], scores, MASK_VALUE)
        weights = jnp.exp(scores - block_sums[..., None])
        weight_grad = jnp.einsum(
            "qhe,khe->hqk", grad_block, value_item, preferred_element_type=jnp.float32
        )
        row_dot = jnp.sum(weight_grad * weights, axis=-1, keepdims=True)
        score_grad = (weights * (weight_grad - row_dot)).astype(jnp.bfloat16)
        query_grad = (
            jnp.einsum("hqk,khe->qhe", score_grad, key_item, preferred_element_type=jnp.float32)
            * score_scale
        )
        key_grad = (
            key_grad
            + jnp.einsum(
                "hqk,qhe->khe", score_grad, query_block, preferred_element_type=jnp.float32
            )
            * score_scale
        )
        value_grad = value_grad + jnp.einsum(
            "hqk,qhe->khe",
            weights.astype(jnp.bfloat16),
            grad_block,
            preferred_element_type=jnp.float32,
        )
        return ((key_grad, value_grad), query_grad)

    offsets = jnp.arange(capacity // block_rows) * block_rows
    zero_rows = jnp.zeros(key_item.shape, jnp.float32)
    (key_grad, value_grad), query_grad = lax.scan(
        one_block, (zero_rows, zero_rows), (offsets, log_sums)
    )
    return (query_grad.reshape(key_item.shape), key_grad, value_grad)


def shards(
    tokens,
    lengths,
    qkv_weight,
    qkv_bias,
    out_weight,
    out_bias,
    norm1_gain,
    norm1_shift,
    up_weight,
    up_bias,
    down_weight,
    down_bias,
    norm2_gain,
    norm2_shift,
    cotangent,
):
    narrow_size = lax.axis_size("narrow")
    slot_dev, capacity, features = tokens.shape
    group_heads = HEADS // narrow_size
    score_scale = HD ** (-0.5)
    block_rows = min(capacity, 512)
    cosine, sine = rotary_tables(capacity, HD)
    all_lengths = lengths.reshape(-1)
    gain_one = norm1_gain.astype(jnp.float32)
    shift_one = norm1_shift.astype(jnp.float32)
    gain_two = norm2_gain.astype(jnp.float32)
    shift_two = norm2_shift.astype(jnp.float32)
    qkv_local, qkv_bias_local, out_local = (qkv_weight, qkv_bias, out_weight)
    up_local, up_bias_local, down_local = (up_weight, up_bias, down_weight)
    row_tokens = lax.all_gather(tokens, "narrow", axis=0, tiled=True)
    slot_count = row_tokens.shape[0]
    projected = jnp.einsum(
        "scd,dje->scje", row_tokens, qkv_local, preferred_element_type=jnp.float32
    ) + qkv_bias_local.astype(jnp.float32)
    head_count = projected.shape[3] // HD
    group_count = head_count // group_heads
    head_shape = (slot_count, capacity, head_count, HD)
    queries = rotate(projected[:, :, 0].reshape(head_shape), cosine, sine).astype(jnp.bfloat16)
    key_rows = rotate(projected[:, :, 1].reshape(head_shape), cosine, sine).astype(jnp.bfloat16)
    value_rows = projected[:, :, 2].reshape(head_shape).astype(jnp.bfloat16)
    item_lengths = jnp.repeat(all_lengths, group_count)
    query_items = to_items(queries, group_count)
    key_items = to_items(key_rows, group_count)
    value_items = to_items(value_rows, group_count)

    def forward_item(item):
        return attend_forward(item[0], item[1], item[2], item[3], block_rows, score_scale)

    context_items, log_sums = lax.map(
        forward_item, (query_items, key_items, value_items, item_lengths)
    )
    context = (
        from_items(context_items, group_count)
        .reshape(slot_count, capacity, head_count * HD)
        .astype(jnp.bfloat16)
    )
    attn_terms = jnp.einsum("scd,de->sce", context, out_local, preferred_element_type=jnp.float32)
    attended = lax.psum_scatter(attn_terms, "narrow", scatter_dimension=0, tiled=True)
    own_tokens = tokens.astype(jnp.float32)
    hidden, normed_one, inv_one = norm_forward(
        own_tokens + attended + out_bias.astype(jnp.float32), gain_one, shift_one
    )
    hidden_low = hidden.astype(jnp.bfloat16)
    hidden_rows = lax.all_gather(hidden_low, "narrow", axis=0, tiled=True)
    upward = jnp.einsum(
        "scd,df->scf", hidden_rows, up_local, preferred_element_type=jnp.float32
    ) + up_bias_local.astype(jnp.float32)
    active = jax.nn.gelu(upward, approximate=False).astype(jnp.bfloat16)
    down_terms = jnp.einsum("scf,fd->scd", active, down_local, preferred_element_type=jnp.float32)
    downward = lax.psum_scatter(down_terms, "narrow", scatter_dimension=0, tiled=True)
    output_value, normed_two, inv_two = norm_forward(
        hidden + downward + down_bias.astype(jnp.float32), gain_two, shift_two
    )
    output = output_value.astype(jnp.bfloat16)
    pre_two_grad, gain_two_grad, shift_two_grad = norm_backward(
        cotangent.astype(jnp.float32), normed_two, inv_two, gain_two
    )
    down_bias_grad = jnp.sum(pre_two_grad, axis=(0, 1))
    pre_two_low = pre_two_grad.astype(jnp.bfloat16)
    down_grad_rows = lax.all_gather(pre_two_low, "narrow", axis=0, tiled=True)
    down_grad = jnp.einsum(
        "scf,scd->fd", active, down_grad_rows, preferred_element_type=jnp.float32
    )
    active_grad = jnp.einsum(
        "scd,fd->scf", down_grad_rows, down_local, preferred_element_type=jnp.float32
    )
    ignored_value, gelu_pull = jax.vjp(lambda inner: jax.nn.gelu(inner, approximate=False), upward)
    upward_grad = gelu_pull(active_grad)[0]
    up_bias_grad = jnp.sum(upward_grad, axis=(0, 1))
    upward_low = upward_grad.astype(jnp.bfloat16)
    up_grad = jnp.einsum("scd,scf->df", hidden_rows, upward_low, preferred_element_type=jnp.float32)
    hidden_terms = jnp.einsum(
        "scf,df->scd", upward_low, up_local, preferred_element_type=jnp.float32
    )
    hidden_grad = lax.psum_scatter(hidden_terms, "narrow", scatter_dimension=0, tiled=True)
    pre_one_grad, gain_one_grad, shift_one_grad = norm_backward(
        hidden_grad + pre_two_grad, normed_one, inv_one, gain_one
    )
    out_bias_grad = jnp.sum(pre_one_grad, axis=(0, 1))
    pre_one_low = pre_one_grad.astype(jnp.bfloat16)
    out_grad_rows = lax.all_gather(pre_one_low, "narrow", axis=0, tiled=True)
    out_grad = jnp.einsum("scd,sce->de", context, out_grad_rows, preferred_element_type=jnp.float32)
    context_grad = jnp.einsum(
        "sce,de->scd", out_grad_rows, out_local, preferred_element_type=jnp.float32
    ).astype(jnp.bfloat16)
    grad_items = to_items(context_grad.reshape(head_shape), group_count)

    def backward_item(item):
        return attend_backward(
            item[0], item[1], item[2], item[3], item[4], item[5], block_rows, score_scale
        )

    query_grad, key_grad, value_grad = lax.map(
        backward_item, (query_items, key_items, value_items, grad_items, log_sums, item_lengths)
    )
    flat_shape = (slot_count, capacity, head_count * HD)
    query_grad = rotate(from_items(query_grad, group_count), cosine, -sine).reshape(flat_shape)
    key_grad = rotate(from_items(key_grad, group_count), cosine, -sine).reshape(flat_shape)
    value_grad = from_items(value_grad, group_count).reshape(flat_shape)
    projected_grad = jnp.stack([query_grad, key_grad, value_grad], axis=2)
    qkv_bias_grad = jnp.sum(projected_grad, axis=(0, 1))
    projected_low = projected_grad.astype(jnp.bfloat16)
    qkv_grad = jnp.einsum(
        "scd,scje->dje", row_tokens, projected_low, preferred_element_type=jnp.float32
    )
    input_terms = jnp.einsum(
        "scje,dje->scd", projected_low, qkv_local, preferred_element_type=jnp.float32
    )
    input_part = lax.psum_scatter(
        input_terms.astype(jnp.bfloat16), "narrow", scatter_dimension=0, tiled=True
    ).astype(jnp.float32)
    input_grad = input_part + pre_one_grad
    small_grads = lax.psum(
        (
            gain_one_grad,
            shift_one_grad,
            gain_two_grad,
            shift_two_grad,
            out_bias_grad,
            down_bias_grad,
        ),
        "narrow",
    )
    summed = lax.psum(
        (
            qkv_grad,
            qkv_bias_grad,
            out_grad,
            small_grads[4],
            small_grads[0],
            small_grads[1],
            up_grad,
            up_bias_grad,
            down_grad,
            small_grads[5],
            small_grads[2],
            small_grads[3],
        ),
        "wide",
    )
    return (
        output,
        input_grad,
        summed[0],
        summed[1],
        summed[2],
        summed[3],
        summed[4],
        summed[5],
        summed[6],
        summed[7],
        summed[8],
        summed[9],
        summed[10],
        summed[11],
    )


def solution(mesh):
    placed = (
        P(("wide", "narrow"), None, None),
        P("wide", None),
        P(None, None, "narrow"),
        P(None, "narrow"),
        P("narrow", None),
        P(),
        P(),
        P(),
        P(None, "narrow"),
        P("narrow"),
        P("narrow", None),
        P(),
        P(),
        P(),
        P(("wide", "narrow"), None, None),
    )
    return jax.shard_map(
        shards,
        mesh=mesh,
        in_specs=placed,
        out_specs=(
            P(("wide", "narrow"), None, None),
            P(("wide", "narrow"), None, None),
            P(None, None, "narrow"),
            P(None, "narrow"),
            P("narrow", None),
            P(),
            P(),
            P(),
            P(None, "narrow"),
            P("narrow"),
            P("narrow", None),
            P(),
            P(),
            P(),
        ),
        check_vma=False,
    )
```

profile of v0, /device:TPU:0, one launch (start us, length us, event | category | flops | bytes accessed | tf_op | source)
XLA Modules:
  0.0 2778.9 jit_solution(16459754968414012674)
XLA Ops:
  11.8 167.4 %all-gather.5.cloned.1.call-done = bf16[4,1536,768]{2,1,0:T(8,128)(2,1)} async-done(((bf16[1,1536,768]{2,1,0:T(8,128)(2,1)}), bf16[4,1536,768]{2,1,0:T(8,128)(2,1)}) %all-gather.5.cloned.1.call-update) | async-done | bytes 9437200 | tf_op jit(solution)/shard_map/all_gather | solution.py:167
  204.4 152.3 %while.61 = (s32[]{:T(128)}, bf16[4,1536,3,64]{1,3,2,0:T(8,128)(2,1)}, f32[4,3,3,512]{3,2,1,0:T(4,128)}, bf16[4,1536,3,64]{1,3,2,0:T(8,128)(2,1)}, bf16[4,1536,3...) while((s32[]{:T(128)}, ...), condition=%wide.region_5.6_spmd.clone, body=%wide.region_0.5_spmd.sunk.clone | while | flops 632291328 | bytes 37272460 | solution.py:186
  207.4 30.9 %while.60 = (s32[]{:T(128)}, bf16[3,512,3,64]{1,3,2,0:T(8,128)(2,1)S(1)}, f32[3,3,512]{2,1,0:T(4,128)}, s32[3]{0:T(128)S(1)}, bf16[1536,3,64]{0,2,1:T(8,128)(2,1...) while((s32[]{:T(128)}, ...), condition=%wide.region_4.4_spmd.clone, body=%wide.region_1.3_spmd.clone.sunk | while | flops 632291328 | bytes 30144168 | solution.py:84
  245.5 30.9 %while.60 = (s32[]{:T(128)}, bf16[3,512,3,64]{1,3,2,0:T(8,128)(2,1)S(1)}, f32[3,3,512]{2,1,0:T(4,128)}, s32[3]{0:T(128)S(1)}, bf16[1536,3,64]{0,2,1:T(8,128)(2,1...) while((s32[]{:T(128)}, ...), condition=%wide.region_4.4_spmd.clone, body=%wide.region_1.3_spmd.clone.sunk | while | flops 632291328 | bytes 30144168 | solution.py:84
  283.5 30.9 %while.60 = (s32[]{:T(128)}, bf16[3,512,3,64]{1,3,2,0:T(8,128)(2,1)S(1)}, f32[3,3,512]{2,1,0:T(4,128)}, s32[3]{0:T(128)S(1)}, bf16[1536,3,64]{0,2,1:T(8,128)(2,1...) while((s32[]{:T(128)}, ...), condition=%wide.region_4.4_spmd.clone, body=%wide.region_1.3_spmd.clone.sunk | while | flops 632291328 | bytes 30144168 | solution.py:84
  321.6 30.9 %while.60 = (s32[]{:T(128)}, bf16[3,512,3,64]{1,3,2,0:T(8,128)(2,1)S(1)}, f32[3,3,512]{2,1,0:T(4,128)}, s32[3]{0:T(128)S(1)}, bf16[1536,3,64]{0,2,1:T(8,128)(2,1...) while((s32[]{:T(128)}, ...), condition=%wide.region_4.4_spmd.clone, body=%wide.region_1.3_spmd.clone.sunk | while | flops 632291328 | bytes 30144168 | solution.py:84
  368.2 311.4 %reduce-scatter.5.cloned.1.call-done = f32[1,1536,768]{2,1,0:T(8,128)} async-done(((f32[4,1536,768]{2,1,0:T(8,128)}), f32[1,1536,768]{2,1,0:T(8,128)}) %reduce-scatter.5.cloned.1.call-update) | async-done | bytes 4718608 | tf_op jit(solution)/shard_map/reduce_scatter | solution.py:195
  687.0 167.9 %all-gather.7.cloned.1.call-done = bf16[4,1536,768]{2,1,0:T(8,128)(2,1)} async-done(((bf16[1,1536,768]{2,1,0:T(8,128)(2,1)}), bf16[4,1536,768]{2,1,0:T(8,128)(2,1)}) %all-gather.7.cloned.1.call-update) | async-done | bytes 9437200 | tf_op jit(solution)/shard_map/all_gather | solution.py:201
  855.0 19.3 fusion.62
  874.3 46.0 %multiply_convert_fusion.1 = (bf16[4,1536,768]{2,1,0:T(8,128)(2,1)S(1)}, f32[4,1536,768]{2,1,0:T(8,128)}) fusion(f32[4,1536,768]{2,1,0:T(8,128)} %get-tuple-element.438, f32[768]{0:T(1024)S(1)} %convert_element_type.166, u8[1536,768]{1,0:T(8,128)(4,1)S(1)} %get-tuple-element.302, u8[1536,768]{1,0:T(8,128)(4,1)S(1)} %get-tuple-element.301), kind=kLoop, calls=%fused_computation.65 | loop fusion | flops 335020032 | bytes 49548288 | tf_op jit(solution)/shard_map/convert_element_type | solution.py:205
  935.2 311.4 %reduce-scatter.7.cloned.1.call-done = f32[1,1536,768]{2,1,0:T(8,128)} async-done(((f32[4,1536,768]{2,1,0:T(8,128)}), f32[1,1536,768]{2,1,0:T(8,128)}) %reduce-scatter.7.cloned.1.call-update) | async-done | bytes 4718608 | tf_op jit(solution)/shard_map/reduce_scatter | solution.py:207
  1263.6 168.0 %all-gather.9.cloned.1.call-done = bf16[4,1536,768]{2,1,0:T(8,128)(2,1)} async-done(((bf16[1,1536,768]{2,1,0:T(8,128)(2,1)}), bf16[4,1536,768]{2,1,0:T(8,128)(2,1)}) %all-gather.9.cloned.1.call-update) | async-done | bytes 9437200 | tf_op jit(solution)/shard_map/all_gather | solution.py:217
  1431.6 25.3 fusion.91
  1471.3 312.1 %reduce-scatter.9.cloned.1.call-done = f32[1,1536,768]{2,1,0:T(8,128)} async-done(((f32[4,1536,768]{2,1,0:T(8,128)}), f32[1,1536,768]{2,1,0:T(8,128)}) %reduce-scatter.9.cloned.1.call-update) | async-done | bytes 4718608 | tf_op jit(solution)/shard_map/reduce_scatter | solution.py:232
  1798.7 168.0 %all-gather.11.cloned.1.call-done = bf16[4,1536,768]{2,1,0:T(8,128)(2,1)} async-done(((bf16[1,1536,768]{2,1,0:T(8,128)(2,1)}), bf16[4,1536,768]{2,1,0:T(8,128)(2,1)}) %all-gather.11.cloned.1.call-update) | async-done | bytes 9437200 | tf_op jit(solution)/shard_map/all_gather | solution.py:238
  1979.2 481.4 %while.63 = (s32[]{:T(128)}, f32[4,1536,3,64]{1,3,2,0:T(8,128)}, f32[4,1536,3,64]{1,3,2,0:T(8,128)}, f32[4,1536,3,64]{1,3,2,0:T(8,128)}, f32[4,3,3,512]{3,2,1,0:...) while((s32[]{:T(128)}, f32[4,1536,3,64]{1,3,2,0:T(8,128)}, ...), condition=%wide.region_21.22_spmd.clone, body=%wide.region_17.21_spmd.sunk.clone | while | flops 1532755968 | bytes 175250576 | solution.py:250
  1986.7 104.4 %while.62 = (s32[]{:T(128)}, f32[1536,3,64]{0,2,1:T(8,128)S(1)}, f32[1536,3,64]{0,2,1:T(8,128)S(1)}, f32[3,512,3,64]{1,3,2,0:T(8,128)}, s32[3]{0:T(128)S(1)}, /*...) while((s32[]{:T(128)}, f32[1536,3,64]{0,2,1:T(8,128)S(1)}, ...), condition=%wide.region_20.20_spmd.clone, body=%wide.region_18.19_spmd.clone.sunk | while | flops 1532755968 | bytes 135104288 | solution.py:131
  2107.1 104.4 %while.62 = (s32[]{:T(128)}, f32[1536,3,64]{0,2,1:T(8,128)S(1)}, f32[1536,3,64]{0,2,1:T(8,128)S(1)}, f32[3,512,3,64]{1,3,2,0:T(8,128)}, s32[3]{0:T(128)S(1)}, /*...) while((s32[]{:T(128)}, f32[1536,3,64]{0,2,1:T(8,128)S(1)}, ...), condition=%wide.region_20.20_spmd.clone, body=%wide.region_18.19_spmd.clone.sunk | while | flops 1532755968 | bytes 135104288 | solution.py:131
  2227.3 104.4 %while.62 = (s32[]{:T(128)}, f32[1536,3,64]{0,2,1:T(8,128)S(1)}, f32[1536,3,64]{0,2,1:T(8,128)S(1)}, f32[3,512,3,64]{1,3,2,0:T(8,128)}, s32[3]{0:T(128)S(1)}, /*...) while((s32[]{:T(128)}, f32[1536,3,64]{0,2,1:T(8,128)S(1)}, ...), condition=%wide.region_20.20_spmd.clone, body=%wide.region_18.19_spmd.clone.sunk | while | flops 1532755968 | bytes 135104288 | solution.py:131
  2347.6 104.4 %while.62 = (s32[]{:T(128)}, f32[1536,3,64]{0,2,1:T(8,128)S(1)}, f32[1536,3,64]{0,2,1:T(8,128)S(1)}, f32[3,512,3,64]{1,3,2,0:T(8,128)}, s32[3]{0:T(128)S(1)}, /*...) while((s32[]{:T(128)}, f32[1536,3,64]{0,2,1:T(8,128)S(1)}, ...), condition=%wide.region_20.20_spmd.clone, body=%wide.region_18.19_spmd.clone.sunk | while | flops 1532755968 | bytes 135104288 | solution.py:131
  2527.4 19.0 all-reduce.2
  2552.4 23.8 all-reduce
  2576.2 68.3 %reduce-scatter.11.cloned.1.call-done = bf16[1,1536,768]{2,1,0:T(8,128)(2,1)} async-done(((bf16[4,1536,768]{2,1,0:T(8,128)(2,1)}), bf16[1,1536,768]{2,1,0:T(8,128)(2,1)}) %reduce-scatter.11.cloned.1.call-update) | async-done | bytes 2359312 | tf_op jit(solution)/shard_map/reduce_scatter | solution.py:266
  2650.3 113.9 %all-reduce.5.cloned.1.call-done = (f32[768,3,192]{0,2,1:T(8,128)}, f32[192,768]{1,0:T(8,128)}, f32[768,768]{1,0:T(8,128)}, f32[768,768]{1,0:T(8,128)}) async-done(((f32[768,3,192]{0,2,1:T(8,128)}, f32[192,768]{1,0:T(8,128)}, f32[768,768]{1,0:T(8,128)}, f32[768,768]{1,0:T(8,128)}), (f32[768,3,192]{0,2,1:T(8,128)}, f32[192,768]{1,0:T(8,128)}, f32[768,768]{1,0:T(8,128)}, ...) | async-done | bytes 7077904 | tf_op jit(solution)/shard_map/psum | solution.py:281
  (521 shorter events, 793.3 us)
Async XLA Ops:
  7.2 847.8 %copy-start = (bf16[768,768]{1,0:T(8,128)(2,1)S(1)}, bf16[768,768]{1,0:T(8,128)(2,1)}, u32[]{:S(2)}) copy-start(bf16[768,768]{1,0:T(8,128)(2,1)} %param.31) | copy-start | bytes 3538948
  7.2 171.9 %copy-start.36 = (bf16[768,3,192]{0,2,1:T(8,128)(2,1)S(1)}, bf16[768,3,192]{0,2,1:T(8,128)(2,1)}, u32[]{:S(2)}) copy-start(bf16[768,3,192]{0,2,1:T(8,128)(2,1)} %param.25) | copy-start | bytes 2654212
  7.2 171.9 %all-gather.5.cloned.1.call-start = ((), (), s32[]{:S(2)}) async-start(), calls=%async_computation.4 | async-start | bytes 11796480 | tf_op jit(solution)/shard_map/all_gather | solution.py:167
  7.9 671.7 %reduce-scatter.5.cloned.1.call-start = ((), (), s32[]{:S(2)}) async-start(), calls=%async_computation.5 | async-start | bytes 23592960 | tf_op jit(solution)/shard_map/reduce_scatter | solution.py:195
  11.8 188.6 %copy-start.19 = (f32[1536,32]{0,1:T(8,128)}, f32[1536,32]{0,1:T(8,128)S(1)}, u32[]{:S(2)}) copy-start(f32[1536,32]{0,1:T(8,128)S(1)} %get-tuple-element.437) | copy-start | bytes 589828
  367.5 312.2 %copy-start.13 = (bf16[1,1536,768]{2,1,0:T(8,128)(2,1)S(1)}, bf16[1,1536,768]{2,1,0:T(8,128)(2,1)}, u32[]{:S(2)}) copy-start(bf16[1,1536,768]{2,1,0:T(8,128)(2,1)} %param.23) | copy-start | bytes 7077892
  367.5 487.5 %all-gather.7.cloned.1.call-start = ((), (), s32[]{:S(2)}) async-start(), calls=%async_computation.6 | async-start | bytes 11796480 | tf_op jit(solution)/shard_map/all_gather | solution.py:201
  686.9 559.7 %reduce-scatter.7.cloned.1.call-start = ((), (), s32[]{:S(2)}) async-start(), calls=%async_computation.7 | async-start | bytes 23592960 | tf_op jit(solution)/shard_map/reduce_scatter | solution.py:207
  874.3 49.7 %copy-start.35 = (bf16[768,768]{1,0:T(8,128)(2,1)S(1)}, bf16[768,768]{1,0:T(8,128)(2,1)}, u32[]{:S(2)}) copy-start(bf16[768,768]{1,0:T(8,128)(2,1)} %param.33) | copy-start | bytes 3538948
  934.5 497.1 %all-gather.9.cloned.1.call-start = ((), (), s32[]{:S(2)}) async-start(), calls=%async_computation.8 | async-start | bytes 11796480 | tf_op jit(solution)/shard_map/all_gather | solution.py:217
  1263.6 519.8 %reduce-scatter.9.cloned.1.call-start = ((), (), s32[]{:S(2)}) async-start(), calls=%async_computation.9 | async-start | bytes 23592960 | tf_op jit(solution)/shard_map/reduce_scatter | solution.py:232
  1471.3 495.4 %all-gather.11.cloned.1.call-start = ((), (), s32[]{:S(2)}) async-start(), calls=%async_computation.10 | async-start | bytes 11796480 | tf_op jit(solution)/shard_map/all_gather | solution.py:238
  1797.0 169.7 %copy-start.20 = (bf16[192,768]{1,0:T(8,128)(2,1)S(1)}, bf16[192,768]{1,0:T(8,128)(2,1)}, u32[]{:S(2)}) copy-start(bf16[192,768]{1,0:T(8,128)(2,1)} %param.27) | copy-start | bytes 884740
  1798.7 845.9 %reduce-scatter.11.cloned.1.call-start = ((), (), s32[]{:S(2)}) async-start(), calls=%async_computation.11 | async-start | bytes 11796480 | tf_op jit(solution)/shard_map/reduce_scatter | solution.py:266
  2483.9 280.3 %all-reduce.5.cloned.1.call-start = ((), (), s32[]{:S(2)}) async-start(), calls=%async_computation.12 | async-start | bytes 14155776 | tf_op jit(solution)/shard_map/psum | solution.py:281
  2484.0 35.7 %slice-start = ((s8[4718592]{0:T(1024)(128)(4,1)}), s8[4194304]{0:T(1024)(128)(4,1)S(1)}, s32[]{:S(2)}) async-start(s8[4718592]{0:T(1024)(128)(4,1)} %bitcast.204), calls=%async_computation.13 | async-start | bytes 8388608
  2484.0 35.7 %slice-start.2 = ((s8[4718592]{0:T(1024)(128)(4,1)}), s8[4194304]{0:T(1024)(128)(4,1)S(1)}, s32[]{:S(2)}) async-start(s8[4718592]{0:T(1024)(128)(4,1)} %bitcast.209), calls=%async_computation.15 | async-start | bytes 8388608
  2484.0 35.7 %slice-start.6 = ((s8[4718592]{0:T(1024)(128)(4,1)}), s8[4194304]{0:T(1024)(128)(4,1)S(1)}, s32[]{:S(2)}) async-start(s8[4718592]{0:T(1024)(128)(4,1)} %bitcast.216), calls=%async_computation.19 | async-start | bytes 8388608
  2484.0 35.7 %slice-start.8 = ((s8[9437184]{0:T(1024)(128)(4,1)}), s8[4194304]{0:T(1024)(128)(4,1)S(1)}, s32[]{:S(2)}) async-start(s8[9437184]{0:T(1024)(128)(4,1)} %bitcast.222), calls=%async_computation.21 | async-start | bytes 8388608
  2484.0 35.7 %slice-start.9 = ((s8[9437184]{0:T(1024)(128)(4,1)}), s8[4194304]{0:T(1024)(128)(4,1)S(1)}, s32[]{:S(2)}) async-start(s8[9437184]{0:T(1024)(128)(4,1)} %bitcast.222), calls=%async_computation.22 | async-start | bytes 8388608
  2499.1 20.6 slice-start.1
  2499.1 20.6 slice-start.3
  2499.1 20.6 slice-start.7
  2499.2 20.6 slice-start.10
  (67 other events, 277.2 us)
Sparse Core Ops, SparseCore 0:
  9.6 169.4 all-gather.4
  367.6 311.9 reduce-scatter.4
  687.1 167.8 all-gather.6
  934.6 311.9 reduce-scatter.6
  1263.7 167.8 all-gather.8
  1471.4 311.9 reduce-scatter.8
  1798.8 167.8 all-gather.10
  2484.0 160.5 reduce-scatter.10
  2649.9 114.2 all-reduce.4
where the time goes:
time: 2790 us; the launch traced here: 2780 us
  waiting for transfers between devices  1790 us (64%)
  matrix products  459 us (16%)
  other arithmetic  266 us (10%)
  local copies, waits for them, and re-layouts  158 us (6%)
  loops' own time  49.1 us (2%)
  blocking collectives  42.9 us (2%)
    reduce_scatter x1, waiting for transfers between devices, shards(): lax.psum_scatter(hidden_terms, 'narrow', scatter_dimension=0, tiled=True)  312 us
    reduce_scatter x1, waiting for transfers between devices, shards(): lax.psum_scatter(attn_terms, 'narrow', scatter_dimension=0, tiled=True)  311 us
    reduce_scatter x1, waiting for transfers between devices, shards(): lax.psum_scatter(down_terms, 'narrow', scatter_dimension=0, tiled=True)  311 us
    all_gather x1, waiting for transfers between devices, shards(): down_grad_rows = lax.all_gather(pre_two_low, 'narrow', axis=0, tiled=True)  168 us
    all_gather x1, waiting for transfers between devices, shards(): out_grad_rows = lax.all_gather(pre_one_low, 'narrow', axis=0, tiled=True)  168 us
    all_gather x1, waiting for transfers between devices, shards(): hidden_rows = lax.all_gather(hidden_low, 'narrow', axis=0, tiled=True)  168 us
    all_gather x1, waiting for transfers between devices, shards(): row_tokens = lax.all_gather(tokens, 'narrow', axis=0, tiled=True)  167 us
    psum x1, waiting for transfers between devices, shards(): lax.psum((qkv_grad, qkv_bias_grad, out_grad, small_grads[4], small_grads[...  114 us
  transfers between devices with their start and end apart: 9, of which 9 were waited for; matrix products, arithmetic and copies ran while one was open for 2% of the time, Pallas kernels for 0%

commit v1 on v0

--- a/solution.py
+++ b/solution.py
@@ -7,6 +7,26 @@
 HD = 64
 NORM_EPS = 1e-06
 MASK_VALUE = -1000000000.0
+
+
+def cells_proceed(x_in, at_axis):
+    x_in = jnp.moveaxis(x_in, 0, at_axis)
+    step_out = x_in.shape
+    return x_in.reshape(
+        *step_out[:at_axis], step_out[at_axis] * step_out[at_axis + 1], *step_out[at_axis + 2 :]
+    )
+
+
+def _unite_scenes(my_data, row_axis):
+    parts_n = lax.axis_size(row_axis)
+    newest = my_data[None]
+    for w in range(parts_n.bit_length() - 1):
+        r1 = 1 << w
+        piece_now = lax.ppermute(newest, row_axis, [(u, u ^ r1) for u in range(parts_n)])
+        part_next = jnp.stack([newest, piece_now])
+        near = lax.axis_index(row_axis) >> w & 1
+        newest = jnp.where(near == 0, part_next, part_next[::-1]).reshape(-1, *my_data.shape)
+    return newest
 
 
 def rotary_tables(capacity, head_dim):
@@ -164,7 +184,11 @@
     shift_two = norm2_shift.astype(jnp.float32)
     qkv_local, qkv_bias_local, out_local = (qkv_weight, qkv_bias, out_weight)
     up_local, up_bias_local, down_local = (up_weight, up_bias, down_weight)
-    row_tokens = lax.all_gather(tokens, "narrow", axis=0, tiled=True)
+
+    def _edit_quotas(u_in, xin, dim_at):
+        return cells_proceed(_unite_scenes(u_in, xin), dim_at)
+
+    row_tokens = _edit_quotas(tokens, "narrow", 0)
     slot_count = row_tokens.shape[0]
     projected = jnp.einsum(
         "scd,dje->scje", row_tokens, qkv_local, preferred_element_type=jnp.float32

time: 2790 us -> 2910 us (1.043)
  waiting for transfers between devices: 1790 us -> 1870 us
    ppermute x0 -> x2, waiting for transfers between devices: none -> 251 us  [_unite_scenes(): lax.ppermute(newest, row_axis, [(u, u ^ r1) for u in range(parts_n)])]
    all_gather x1 -> x0, waiting for transfers between devices: 167 us -> none  [shards(): row_tokens = lax.all_gather(tokens, 'narrow', axis=0, tiled=True)]
  transfers between devices with their start and end apart: 9 -> 10, of which waited for: 9 -> 10; matrix products, arithmetic and copies ran while one was open for 2% -> 2% of each run, Pallas kernels for 0% -> 0%
where the time goes in v1:
time: 2910 us; the launch traced here: 2900 us
  waiting for transfers between devices  1870 us (64%)
  matrix products  463 us (16%)
  other arithmetic  291 us (10%)
  local copies, waits for them, and re-layouts  158 us (5%)
  loops' own time  49.6 us (2%)
  blocking collectives  42.2 us (1%)
    reduce_scatter x1, waiting for transfers between devices, shards(): lax.psum_scatter(attn_terms, 'narrow', scatter_dimension=0, tiled=True)  314 us
    reduce_scatter x1, waiting for transfers between devices, shards(): lax.psum_scatter(hidden_terms, 'narrow', scatter_dimension=0, tiled=True)  312 us
    reduce_scatter x1, waiting for transfers between devices, shards(): lax.psum_scatter(down_terms, 'narrow', scatter_dimension=0, tiled=True)  311 us
    ppermute x2, waiting for transfers between devices, _unite_scenes(): lax.ppermute(newest, row_axis, [(u, u ^ r1) for u in range(parts_n)])  251 us
    all_gather x1, waiting for transfers between devices, shards(): down_grad_rows = lax.all_gather(pre_two_low, 'narrow', axis=0, tiled=True)  168 us
    all_gather x1, waiting for transfers between devices, shards(): out_grad_rows = lax.all_gather(pre_one_low, 'narrow', axis=0, tiled=True)  168 us
    all_gather x1, waiting for transfers between devices, shards(): hidden_rows = lax.all_gather(hidden_low, 'narrow', axis=0, tiled=True)  168 us
    psum x1, waiting for transfers between devices, shards(): lax.psum((qkv_grad, qkv_bias_grad, out_grad, small_grads[4], small_grads[...  114 us
  transfers between devices with their start and end apart: 10, of which 10 were waited for; matrix products, arithmetic and copies ran while one was open for 2% of the time, Pallas kernels for 0%

profile of v1, /device:TPU:0, one launch (start us, length us, event | category | flops | bytes accessed | tf_op | source)
XLA Modules:
  0.0 2897.5 jit_solution(979373673239033721)
XLA Ops:
  10.3 51.5 %collective-permute-done = bf16[1,1,1536,768]{3,2,1,0:T(8,128)(2,1)S(1)} collective-permute-done((bf16[1,1,1536,768]{3,2,1,0:T(8,128)(2,1)}, bf16[1,1,1536,768]{3,2,1,0:T(8,128)(2,1)S(1)}, u32[]{:S(2)}, u32[]{:S(2)}) %collective-permute-start) | collective-permute-done | bytes 2359328 | tf_op jit(solution)/shard_map/ppermute | solution.py:25
  74.5 199.5 %collective-permute-done.1 = bf16[2,1,1536,768]{3,2,0,1:T(8,128)(2,1)} collective-permute-done((bf16[2,1,1536,768]{3,2,0,1:T(8,128)(2,1)}, bf16[2,1,1536,768]{3,2,0,1:T(8,128)(2,1)}, u32[]{:S(2)}, u32[]{:S(2)}) %collective-permute-start.1) | collective-permute-done | bytes 4718624 | tf_op jit(solution)/shard_map/ppermute | solution.py:25
  320.2 152.3 %while.61 = (s32[]{:T(128)}, bf16[4,1536,3,64]{1,3,2,0:T(8,128)(2,1)}, f32[4,3,3,512]{3,2,1,0:T(4,128)}, bf16[4,1536,3,64]{1,3,2,0:T(8,128)(2,1)}, bf16[4,1536,3...) while((s32[]{:T(128)}, ...), condition=%wide.region_5.6_spmd.clone, body=%wide.region_0.5_spmd.sunk.clone | while | flops 632291328 | bytes 37272460 | solution.py:210
  323.3 30.9 %while.60 = (s32[]{:T(128)}, bf16[3,512,3,64]{1,3,2,0:T(8,128)(2,1)S(1)}, f32[3,3,512]{2,1,0:T(4,128)}, s32[3]{0:T(128)S(1)}, bf16[1536,3,64]{0,2,1:T(8,128)(2,1...) while((s32[]{:T(128)}, ...), condition=%wide.region_4.4_spmd.clone, body=%wide.region_1.3_spmd.clone.sunk | while | flops 632291328 | bytes 30144168 | solution.py:104
  361.3 30.9 %while.60 = (s32[]{:T(128)}, bf16[3,512,3,64]{1,3,2,0:T(8,128)(2,1)S(1)}, f32[3,3,512]{2,1,0:T(4,128)}, s32[3]{0:T(128)S(1)}, bf16[1536,3,64]{0,2,1:T(8,128)(2,1...) while((s32[]{:T(128)}, ...), condition=%wide.region_4.4_spmd.clone, body=%wide.region_1.3_spmd.clone.sunk | while | flops 632291328 | bytes 30144168 | solution.py:104
  399.4 30.9 %while.60 = (s32[]{:T(128)}, bf16[3,512,3,64]{1,3,2,0:T(8,128)(2,1)S(1)}, f32[3,3,512]{2,1,0:T(4,128)}, s32[3]{0:T(128)S(1)}, bf16[1536,3,64]{0,2,1:T(8,128)(2,1...) while((s32[]{:T(128)}, ...), condition=%wide.region_4.4_spmd.clone, body=%wide.region_1.3_spmd.clone.sunk | while | flops 632291328 | bytes 30144168 | solution.py:104
  437.5 30.9 %while.60 = (s32[]{:T(128)}, bf16[3,512,3,64]{1,3,2,0:T(8,128)(2,1)S(1)}, f32[3,3,512]{2,1,0:T(4,128)}, s32[3]{0:T(128)S(1)}, bf16[1536,3,64]{0,2,1:T(8,128)(2,1...) while((s32[]{:T(128)}, ...), condition=%wide.region_4.4_spmd.clone, body=%wide.region_1.3_spmd.clone.sunk | while | flops 632291328 | bytes 30144168 | solution.py:104
  484.1 314.2 %reduce-scatter.5.cloned.1.call-done = f32[1,1536,768]{2,1,0:T(8,128)} async-done(((f32[4,1536,768]{2,1,0:T(8,128)}), f32[1,1536,768]{2,1,0:T(8,128)}) %reduce-scatter.5.cloned.1.call-update) | async-done | bytes 4718608 | tf_op jit(solution)/shard_map/reduce_scatter | solution.py:219
  805.7 167.9 %all-gather.4.cloned.1.call-done = bf16[4,1536,768]{2,1,0:T(8,128)(2,1)} async-done(((bf16[1,1536,768]{2,1,0:T(8,128)(2,1)}), bf16[4,1536,768]{2,1,0:T(8,128)(2,1)}) %all-gather.4.cloned.1.call-update) | async-done | bytes 9437200 | tf_op jit(solution)/shard_map/all_gather | solution.py:225
  973.6 19.4 fusion.55
  993.0 45.9 %multiply_convert_fusion.1 = (bf16[4,1536,768]{2,1,0:T(8,128)(2,1)S(1)}, f32[4,1536,768]{2,1,0:T(8,128)}) fusion(f32[4,1536,768]{2,1,0:T(8,128)} %get-tuple-element.440, f32[768]{0:T(1024)S(1)} %convert_element_type.166, u8[1536,768]{1,0:T(8,128)(4,1)S(1)} %get-tuple-element.302, u8[1536,768]{1,0:T(8,128)(4,1)S(1)} %get-tuple-element.301), kind=kLoop, calls=%fused_computation.65 | loop fusion | flops 335020032 | bytes 49548288 | tf_op jit(solution)/shard_map/convert_element_type | solution.py:229
  1053.8 311.4 %reduce-scatter.7.cloned.1.call-done = f32[1,1536,768]{2,1,0:T(8,128)} async-done(((f32[4,1536,768]{2,1,0:T(8,128)}), f32[1,1536,768]{2,1,0:T(8,128)}) %reduce-scatter.7.cloned.1.call-update) | async-done | bytes 4718608 | tf_op jit(solution)/shard_map/reduce_scatter | solution.py:231
  1382.2 168.0 %all-gather.6.cloned.1.call-done = bf16[4,1536,768]{2,1,0:T(8,128)(2,1)} async-done(((bf16[1,1536,768]{2,1,0:T(8,128)(2,1)}), bf16[4,1536,768]{2,1,0:T(8,128)(2,1)}) %all-gather.6.cloned.1.call-update) | async-done | bytes 9437200 | tf_op jit(solution)/shard_map/all_gather | solution.py:241
  1550.2 25.1 fusion.83
  1589.8 312.1 %reduce-scatter.9.cloned.1.call-done = f32[1,1536,768]{2,1,0:T(8,128)} async-done(((f32[4,1536,768]{2,1,0:T(8,128)}), f32[1,1536,768]{2,1,0:T(8,128)}) %reduce-scatter.9.cloned.1.call-update) | async-done | bytes 4718608 | tf_op jit(solution)/shard_map/reduce_scatter | solution.py:256
  1917.2 168.0 %all-gather.8.cloned.1.call-done = bf16[4,1536,768]{2,1,0:T(8,128)(2,1)} async-done(((bf16[1,1536,768]{2,1,0:T(8,128)(2,1)}), bf16[4,1536,768]{2,1,0:T(8,128)(2,1)}) %all-gather.8.cloned.1.call-update) | async-done | bytes 9437200 | tf_op jit(solution)/shard_map/all_gather | solution.py:262
  2097.7 481.3 %while.63 = (s32[]{:T(128)}, f32[4,1536,3,64]{1,3,2,0:T(8,128)}, f32[4,1536,3,64]{1,3,2,0:T(8,128)}, f32[4,1536,3,64]{1,3,2,0:T(8,128)}, f32[4,3,3,512]{3,2,1,0:...) while((s32[]{:T(128)}, f32[4,1536,3,64]{1,3,2,0:T(8,128)}, ...), condition=%wide.region_21.22_spmd.clone, body=%wide.region_17.21_spmd.sunk.clone | while | flops 1532755968 | bytes 175250576 | solution.py:274
  2105.3 104.3 %while.62 = (s32[]{:T(128)}, f32[1536,3,64]{0,2,1:T(8,128)S(1)}, f32[1536,3,64]{0,2,1:T(8,128)S(1)}, f32[3,512,3,64]{1,3,2,0:T(8,128)}, s32[3]{0:T(128)S(1)}, /*...) while((s32[]{:T(128)}, f32[1536,3,64]{0,2,1:T(8,128)S(1)}, ...), condition=%wide.region_20.20_spmd.clone, body=%wide.region_18.19_spmd.clone.sunk | while | flops 1532755968 | bytes 135104288 | solution.py:151
  2225.5 104.3 %while.62 = (s32[]{:T(128)}, f32[1536,3,64]{0,2,1:T(8,128)S(1)}, f32[1536,3,64]{0,2,1:T(8,128)S(1)}, f32[3,512,3,64]{1,3,2,0:T(8,128)}, s32[3]{0:T(128)S(1)}, /*...) while((s32[]{:T(128)}, f32[1536,3,64]{0,2,1:T(8,128)S(1)}, ...), condition=%wide.region_20.20_spmd.clone, body=%wide.region_18.19_spmd.clone.sunk | while | flops 1532755968 | bytes 135104288 | solution.py:151
  2345.8 104.3 %while.62 = (s32[]{:T(128)}, f32[1536,3,64]{0,2,1:T(8,128)S(1)}, f32[1536,3,64]{0,2,1:T(8,128)S(1)}, f32[3,512,3,64]{1,3,2,0:T(8,128)}, s32[3]{0:T(128)S(1)}, /*...) while((s32[]{:T(128)}, f32[1536,3,64]{0,2,1:T(8,128)S(1)}, ...), condition=%wide.region_20.20_spmd.clone, body=%wide.region_18.19_spmd.clone.sunk | while | flops 1532755968 | bytes 135104288 | solution.py:151
  2466.0 104.3 %while.62 = (s32[]{:T(128)}, f32[1536,3,64]{0,2,1:T(8,128)S(1)}, f32[1536,3,64]{0,2,1:T(8,128)S(1)}, f32[3,512,3,64]{1,3,2,0:T(8,128)}, s32[3]{0:T(128)S(1)}, /*...) while((s32[]{:T(128)}, f32[1536,3,64]{0,2,1:T(8,128)S(1)}, ...), condition=%wide.region_20.20_spmd.clone, body=%wide.region_18.19_spmd.clone.sunk | while | flops 1532755968 | bytes 135104288 | solution.py:151
  2673.9 24.3 all-reduce
  2698.2 64.8 %reduce-scatter.11.cloned.1.call-done = bf16[1,1536,768]{2,1,0:T(8,128)(2,1)} async-done(((bf16[4,1536,768]{2,1,0:T(8,128)(2,1)}), bf16[1,1536,768]{2,1,0:T(8,128)(2,1)}) %reduce-scatter.11.cloned.1.call-update) | async-done | bytes 2359312 | tf_op jit(solution)/shard_map/reduce_scatter | solution.py:290
  2768.7 113.9 %all-reduce.5.cloned.1.call-done = (f32[768,3,192]{0,2,1:T(8,128)}, f32[192,768]{1,0:T(8,128)}, f32[768,768]{1,0:T(8,128)}, f32[768,768]{1,0:T(8,128)}) async-done(((f32[768,3,192]{0,2,1:T(8,128)}, f32[192,768]{1,0:T(8,128)}, f32[768,768]{1,0:T(8,128)}, f32[768,768]{1,0:T(8,128)}), (f32[768,3,192]{0,2,1:T(8,128)}, f32[192,768]{1,0:T(8,128)}, f32[768,768]{1,0:T(8,128)}, ...) | async-done | bytes 7077904 | tf_op jit(solution)/shard_map/psum | solution.py:305
  (521 shorter events, 847.1 us)
Async XLA Ops:
  7.2 966.4 %copy-start = (bf16[768,768]{1,0:T(8,128)(2,1)S(1)}, bf16[768,768]{1,0:T(8,128)(2,1)}, u32[]{:S(2)}) copy-start(bf16[768,768]{1,0:T(8,128)(2,1)} %param.31) | copy-start | bytes 3538948
  7.2 791.1 %reduce-scatter.5.cloned.1.call-start = ((), (), s32[]{:S(2)}) async-start(), calls=%async_computation.4 | async-start | bytes 23592960 | tf_op jit(solution)/shard_map/reduce_scatter | solution.py:219
  7.2 54.5 %collective-permute-start = (bf16[1,1,1536,768]{3,2,1,0:T(8,128)(2,1)}, bf16[1,1,1536,768]{3,2,1,0:T(8,128)(2,1)S(1)}, u32[]{:S(2)}, u32[]{:S(2)}) collective-permute-start(bf16[1,1,1536,768]{3,2,1,0:T(8,128)(2,1)} %bitcast.231), channel_id=1, source_target_pairs={{0,1},{1,0},{2,3},{3,2},{4,5},{5,4},{6,7},{7,6},{8,9},{9,8},{10,11... | collective-permute-start | bytes 7077896 | tf_op jit(solution)/shard_map/ppermute | solution.py:25
  63.9 7.5 copy-start.28
  68.7 205.3 %collective-permute-start.1 = (bf16[2,1,1536,768]{3,2,0,1:T(8,128)(2,1)}, bf16[2,1,1536,768]{3,2,0,1:T(8,128)(2,1)}, u32[]{:S(2)}, u32[]{:S(2)}) collective-permute-start(bf16[2,1,1536,768]{3,2,0,1:T(8,128)(2,1)} %get-tuple-element.432), channel_id=1, source_target_pairs={{0,2},{1,3},{2,0},{3,1},{4,6},{5,7},{6,4},{7,5},{8,10},{9,11},{10,... | collective-permute-start | bytes 14155784 | tf_op jit(solution)/shard_map/ppermute | solution.py:25
  74.5 241.7 %copy-start.19 = (f32[1536,32]{0,1:T(8,128)}, f32[1536,32]{0,1:T(8,128)S(1)}, u32[]{:S(2)}) copy-start(f32[1536,32]{0,1:T(8,128)S(1)} %get-tuple-element.439) | copy-start | bytes 589828
  282.3 12.2 copy-start.37
  483.3 315.0 %copy-start.14 = (bf16[1,1536,768]{2,1,0:T(8,128)(2,1)S(1)}, bf16[1,1536,768]{2,1,0:T(8,128)(2,1)}, u32[]{:S(2)}) copy-start(bf16[1,1536,768]{2,1,0:T(8,128)(2,1)} %param.23) | copy-start | bytes 7077892
  483.4 490.2 %all-gather.4.cloned.1.call-start = ((), (), s32[]{:S(2)}) async-start(), calls=%async_computation.5 | async-start | bytes 11796480 | tf_op jit(solution)/shard_map/all_gather | solution.py:225
  805.6 559.6 %reduce-scatter.7.cloned.1.call-start = ((), (), s32[]{:S(2)}) async-start(), calls=%async_computation.6 | async-start | bytes 23592960 | tf_op jit(solution)/shard_map/reduce_scatter | solution.py:231
  993.0 49.6 %copy-start.36 = (bf16[768,768]{1,0:T(8,128)(2,1)S(1)}, bf16[768,768]{1,0:T(8,128)(2,1)}, u32[]{:S(2)}) copy-start(bf16[768,768]{1,0:T(8,128)(2,1)} %param.33) | copy-start | bytes 3538948
  1053.1 497.0 %all-gather.6.cloned.1.call-start = ((), (), s32[]{:S(2)}) async-start(), calls=%async_computation.7 | async-start | bytes 11796480 | tf_op jit(solution)/shard_map/all_gather | solution.py:241
  1382.2 519.7 %reduce-scatter.9.cloned.1.call-start = ((), (), s32[]{:S(2)}) async-start(), calls=%async_computation.8 | async-start | bytes 23592960 | tf_op jit(solution)/shard_map/reduce_scatter | solution.py:256
  1589.7 495.4 %all-gather.8.cloned.1.call-start = ((), (), s32[]{:S(2)}) async-start(), calls=%async_computation.9 | async-start | bytes 11796480 | tf_op jit(solution)/shard_map/all_gather | solution.py:262
  1915.5 169.7 %copy-start.20 = (bf16[192,768]{1,0:T(8,128)(2,1)S(1)}, bf16[192,768]{1,0:T(8,128)(2,1)}, u32[]{:S(2)}) copy-start(bf16[192,768]{1,0:T(8,128)(2,1)} %param.27) | copy-start | bytes 884740
  1917.2 845.8 %reduce-scatter.11.cloned.1.call-start = ((), (), s32[]{:S(2)}) async-start(), calls=%async_computation.10 | async-start | bytes 11796480 | tf_op jit(solution)/shard_map/reduce_scatter | solution.py:290
  2602.3 280.3 %all-reduce.5.cloned.1.call-start = ((), (), s32[]{:S(2)}) async-start(), calls=%async_computation.11 | async-start | bytes 14155776 | tf_op jit(solution)/shard_map/psum | solution.py:305
  2602.3 36.0 %slice-start = ((s8[4718592]{0:T(1024)(128)(4,1)}), s8[4194304]{0:T(1024)(128)(4,1)S(1)}, s32[]{:S(2)}) async-start(s8[4718592]{0:T(1024)(128)(4,1)} %bitcast.212), calls=%async_computation.12 | async-start | bytes 8388608
  2602.4 36.0 %slice-start.2 = ((s8[4718592]{0:T(1024)(128)(4,1)}), s8[4194304]{0:T(1024)(128)(4,1)S(1)}, s32[]{:S(2)}) async-start(s8[4718592]{0:T(1024)(128)(4,1)} %bitcast.217), calls=%async_computation.14 | async-start | bytes 8388608
  2602.4 35.9 %slice-start.6 = ((s8[4718592]{0:T(1024)(128)(4,1)}), s8[4194304]{0:T(1024)(128)(4,1)S(1)}, s32[]{:S(2)}) async-start(s8[4718592]{0:T(1024)(128)(4,1)} %bitcast.224), calls=%async_computation.18 | async-start | bytes 8388608
  2617.5 14.3 copy-start.13
  2617.5 20.8 slice-start.1
  2617.5 20.8 slice-start.3
  2617.5 20.8 slice-start.7
  (66 other events, 263.0 us)
Sparse Core Ops, SparseCore 0:
  483.5 314.7 reduce-scatter.4
  805.7 167.8 all-gather.3
  1053.3 311.9 reduce-scatter.6
  1382.3 167.8 all-gather.5
  1589.9 311.9 reduce-scatter.8
  1917.3 167.8 all-gather.7
  2602.4 160.5 reduce-scatter.10
  2768.3 114.3 all-reduce.4
